TPU v7x, 256 devices: a whole 4x4x8 slice. The times are simulated.
256 devices in a mesh: rows: 64 (over y, z, core), feat: 4 (over x).
Axes of the slice: x: 4, y: 4, z: 8, core: 2. Of those that a mesh axis runs over, the one named last changes fastest.
Arguments:
- feats: bfloat16 [256, 131072], P('feat', 'rows'), may hold values from -6 to 6
- weight: bfloat16 [256, 256], P('feat'), may hold values from -0.375 to 0.375
- bias: float32 [256], P('feat'), may hold values from -3 to 3
- tile_cols: int32 [8192], P('rows'), may hold values from 0 to 1023, as said below
- tile_values: bfloat16 [8192, 128, 128], P('rows'), may hold values from -0.1875 to 0.1875
- cotangent: bfloat16 [256, 131072], P('feat', 'rows'), may hold values from -6 to 6
Outputs:
- hidden_out: bfloat16 [256, 131072], P('feat', 'rows')
- grad_input: float32 [256, 131072], P('feat', 'rows')
- grad_weight: float32 [256, 256], P('feat')
- grad_bias: float32 [256], P('feat')
Inputs may be any that keep to these rules, and one draw needn't show every extreme that they name: `tile_cols`: column blocks of tiles. In each row block the first 4 tiles have column blocks on the same index of rows as the row block (index = column block // 16). Of the other tiles of one index of rows, at most 2 have column blocks on any one index, and in every draw one index receives exactly 2 such tiles from every index.
All inputs are finite; a program needn't handle non-finite values.
Results may differ from a plain program's by a relative error of at most 0.0058.
Values may be sent and summed in bfloat16 or wider, within the bound.
No kernel may reach another device: no remote copies, remote signals or barrier semaphores. Data moves between devices by JAX's collectives and lax.ppermute only.
A program may use at most 128 MiB of HBM per device.

v0:
```python
import math
import jax
import jax.numpy as jnp
from jax import lax
from jax.sharding import PartitionSpec as P

TL = 4


def local(feats, weight, bias, tile_cols, tile_values, cotangent):
    hid_dev = weight.shape[1] // lax.axis_size("feat")
    nodes_dev = feats.shape[1]
    block = tile_values.shape[1]
    row_blocks = nodes_dev // block
    peers = lax.axis_size("rows")
    tiles_dev = tile_cols.shape[0]
    per_block = tiles_dev // row_blocks
    remote_count = row_blocks * (per_block - TL)
    capacity = 2 * remote_count // peers
    num_slots = peers * capacity
    columns = weight
    mixed = lax.psum_scatter(
        lax.dot_general(
            columns, feats, (((0,), (0,)), ((), ())), preferred_element_type=jnp.float32
        ),
        "feat",
        scatter_dimension=0,
        tiled=True,
    )
    proj = mixed.astype(jnp.bfloat16)
    grid = tile_cols.reshape(row_blocks, per_block)
    tiles = tile_values.reshape(row_blocks, per_block, block, block)
    local_tiles = tiles[:, :TL]
    remote_tiles = tiles[:, TL:]
    local_cols = grid[:, :TL] % row_blocks
    remote_cols = grid[:, TL:].reshape(-1)
    remote_owner = remote_cols // row_blocks
    remote_local = remote_cols % row_blocks
    owner_onehot = (remote_owner[:, None] == jnp.arange(peers)[None, :]).astype(jnp.int32)
    before = jnp.cumsum(owner_onehot, axis=0) - owner_onehot
    ranks = jnp.sum(before * owner_onehot, axis=1)
    slots = remote_owner * capacity + ranks
    request = jnp.full((num_slots,), -1, jnp.int32).at[slots].set(remote_local)
    slot_tile = (
        jnp.full((num_slots,), -1, jnp.int32)
        .at[slots]
        .set(jnp.arange(remote_count, dtype=jnp.int32))
    )
    wanted = lax.all_to_all(
        request.reshape(peers, capacity), "rows", split_axis=0, concat_axis=0, tiled=True
    ).reshape(-1)
    gathered = lax.all_gather(proj, "rows", axis=1, tiled=True)
    gathered = gathered.reshape(hid_dev, -1, block)
    fetched = jnp.take(gathered, tile_cols, axis=1).reshape(hid_dev, row_blocks, per_block, block)
    local_part = jnp.einsum(
        "fbtk,btnk->bfn", fetched[:, :, :TL], local_tiles, preferred_element_type=jnp.float32
    )
    remote_part = jnp.einsum(
        "fbtk,btnk->bfn", fetched[:, :, TL:], remote_tiles, preferred_element_type=jnp.float32
    )
    summed = local_part + remote_part
    pre = summed.transpose(1, 0, 2).reshape(hid_dev, nodes_dev) + bias[:, None]
    hidden_out = jax.nn.silu(pre).astype(jnp.bfloat16)
    sigma = jax.nn.sigmoid(pre)
    grad_pre = cotangent.astype(jnp.float32) * (sigma * (1.0 + pre * (1.0 - sigma)))
    bias_part = jnp.sum(grad_pre, axis=1)
    grad_blocks = (
        grad_pre.astype(jnp.bfloat16).reshape(hid_dev, row_blocks, block).transpose(1, 0, 2)
    )
    local_back = jnp.einsum(
        "bfn,btnk->btfk", grad_blocks, local_tiles, preferred_element_type=jnp.float32
    )
    local_onehot = (local_cols[:, :, None] == jnp.arange(row_blocks)[None, None, :]).astype(
        jnp.float32
    )
    grad_proj_blocks = jnp.einsum(
        "bts,btfk->sfk", local_onehot, local_back, precision=lax.Precision.HIGHEST
    )
    remote_back = jnp.einsum(
        "bfn,btnk->btfk", grad_blocks, remote_tiles, preferred_element_type=jnp.float32
    )
    remote_back = remote_back.reshape(remote_count, hid_dev, block)
    filled = (slot_tile >= 0).astype(jnp.float32)
    outgoing_back = remote_back[jnp.maximum(slot_tile, 0)] * filled[:, None, None]
    outgoing_back = outgoing_back.reshape(peers, capacity, hid_dev, block)
    returned = lax.all_to_all(
        outgoing_back, "rows", split_axis=0, concat_axis=0, tiled=True
    ).reshape(num_slots, hid_dev, block)
    wanted_onehot = (wanted[:, None] == jnp.arange(row_blocks)[None, :]).astype(jnp.float32)
    grad_proj_blocks = grad_proj_blocks + jnp.einsum(
        "sb,sfk->bfk", wanted_onehot, returned, precision=lax.Precision.HIGHEST
    )
    grad_proj = grad_proj_blocks.transpose(1, 0, 2).reshape(hid_dev, nodes_dev).astype(jnp.bfloat16)
    piece = lax.all_gather(grad_proj, "feat", axis=0, tiled=True)
    columns = weight
    input_grad = jnp.dot(columns, piece, preferred_element_type=jnp.float32)
    partial_rows = lax.dot_general(
        feats, piece, (((1,), (1,)), ((), ())), preferred_element_type=jnp.float32
    )
    weight_total, bias_total = lax.psum((partial_rows, bias_part), "rows")
    divisor = math.sqrt(nodes_dev * peers)
    return (hidden_out, input_grad, weight_total / divisor, bias_total / divisor)


def solution(mesh):
    placed = (
        P("feat", "rows"),
        P("feat", None),
        P("feat"),
        P("rows"),
        P("rows", None, None),
        P("feat", "rows"),
    )
    return jax.shard_map(
        local,
        mesh=mesh,
        in_specs=placed,
        out_specs=(P("feat", "rows"), P("feat", "rows"), P("feat", None), P("feat")),
        check_vma=False,
    )
```

profile of v0, /device:TPU:1, one launch (start us, length us, event | category | flops | bytes accessed | tf_op | source)
XLA Modules:
  0.0 594.8 jit_solution(7321926682911000968)
XLA Ops:
  7.2 0.0 copy-start
  7.2 0.0 reduce-scatter.2.cloned.1.call-start
  7.2 0.9 copy-done
  8.1 2.6 fusion.50
  10.7 0.0 copy-start.5
  10.7 0.0 reduce-scatter.2.cloned.1.call-update
  10.7 0.0 all-gather.3.cloned.1.call-start
  10.8 36.1 %reduce-scatter.2.cloned.1.call-done = f32[64,2048]{1,0:T(8,128)} async-done(((f32[256,2048]{1,0:T(8,128)}), f32[64,2048]{1,0:T(8,128)}) %reduce-scatter.2.cloned.1.call-update) | async-done | bytes 524304 | tf_op jit(solution)/shard_map/reduce_scatter | solution.py:22
  46.9 1.8 convert_element_type.27
  48.7 0.0 all-gather.3.cloned.1.call-update
  48.7 0.0 copy-done.5
  48.7 0.1 reshape.160
  48.8 0.1 fusion.49
  48.9 0.1 reshape.163
  49.0 0.1 reshape.162
  49.1 0.1 fusion.33
  49.1 0.1 reduce_window_sum.11
  49.2 0.2 select_reduce_fusion
  49.4 0.8 scatter_custom_fusion
  50.2 0.8 all_to_all.9
  51.0 10.6 %all-to-all-start = ((s32[64,1,2]{2,1,0:T(1,128)}), s32[64,1,2]{2,1,0:T(1,128)S(1)}, u32[]{:S(2)}, u32[]{:S(2)}) async-start(s32[64,1,2]{2,1,0:T(1,128)} %bitcast.17), calls=%async_computation.1 | async-start | bytes 65536 | tf_op jit(solution)/shard_map/all_to_all | solution.py:49
  61.6 0.1 broadcast_in_dim.26
  61.7 0.8 scatter_custom_fusion.1
  62.5 0.1 reshape.166
  62.7 88.0 %all-gather.3.cloned.1.call-done = bf16[64,131072]{1,0:T(8,128)(2,1)} async-done(((bf16[64,2048]{1,0:T(8,128)(2,1)}), bf16[64,131072]{1,0:T(8,128)(2,1)}) %all-gather.3.cloned.1.call-update) | async-done | bytes 16777232 | tf_op jit(solution)/shard_map/all_gather | solution.py:52
  150.8 15.3 %copy_bitcast_fusion = bf16[64,1024,128]{2,0,1:T(8,128)(2,1)} fusion(bf16[64,131072]{1,0:T(8,128)(2,1)} %all-gather.3.cloned.1.call-done), kind=kLoop, calls=%fused_computation.4 | loop fusion | bytes 33554432 | tf_op jit(solution)/shard_map/reshape | solution.py:53
  166.0 6.7 %gather_fusion = bf16[128,64,128]{2,1,0:T(8,128)(2,1)S(1)} fusion(bf16[64,1024,128]{2,0,1:T(8,128)(2,1)} %copy_bitcast_fusion, s32[1024]{0:T(1024)S(1)} %pad_clamp_fusion.1), kind=kCustom, calls=%fused_computation | custom fusion | bytes 4194816 | tf_op jit(solution)/shard_map/jit(_take)/gather | solution.py:54
  172.8 0.0 copy-start.1
  172.8 2.6 fusion.16
  175.4 0.2 copy-done.1
  175.6 0.0 copy-start.2
  175.6 0.0 copy-start.4
  175.6 0.9 fusion.25
  176.5 0.0 copy-done.2
  176.5 0.0 copy-done.4
  176.5 1.1 fusion.48
  177.7 0.5 fusion.2
  178.1 2.8 gather_fusion.1
  180.9 2.5 broadcast_multiply_fusion
  183.4 5.8 copy.32
  189.2 0.0 all-to-all-done
  189.2 6.2 %all-to-all-start.1 = ((f32[64,2,64,128]{3,1,2,0:T(2,128)}), f32[64,2,64,128]{3,1,2,0:T(2,128)}, u32[]{:S(2)}, u32[]{:S(2)}) async-start(f32[64,2,64,128]{3,1,2,0:T(2,128)} %copy.32), calls=%async_computation.2 | async-start | bytes 8388608 | tf_op jit(solution)/shard_map/all_to_all | solution.py:86
  195.4 0.2 all-gather.5.cloned.1.call-start
  195.6 0.1 copy.28
  195.7 0.5 broadcast.163
  196.2 0.7 reduce.3
  197.0 0.1 eq.51
  197.1 2.0 fusion.10
  199.1 2.3 fusion.13
  201.4 89.9 %all-to-all-done.1 = f32[64,2,64,128]{3,1,2,0:T(2,128)} async-done(((f32[64,2,64,128]{3,1,2,0:T(2,128)}), f32[64,2,64,128]{3,1,2,0:T(2,128)}, u32[]{:S(2)}, u32[]{:S(2)}) %all-to-all-start.1) | async-done | bytes 4194336 | tf_op jit(solution)/shard_map/all_to_all | solution.py:86
  291.3 4.5 copy.33
  295.8 1.5 fusion.28
  297.3 0.0 copy-start.3
  297.3 0.8 copy.62
  298.1 0.0 all-gather.5.cloned.1.call-update
  298.1 0.0 all-reduce.2.cloned.1.call-start
  298.2 123.7 %psum.15 = f32[64]{0:T(128)S(1)} all-reduce(f32[64]{0:T(128)S(1)} %get-tuple-element.4), channel_id=1, replica_groups=mesh['rows'=64,'feat'=4] {'rows'}, use_global_device_ids=true, to_apply=%region_7.8 | all-reduce | flops 64 | bytes 512 | tf_op jit(solution)/shard_map/psum | solution.py:100
  421.9 0.5 broadcast_multiply_fusion.2
  422.4 2.3 convolution_bitcast_fusion.1
  424.7 0.0 all-reduce.2.cloned.1.call-update
  424.8 0.0 copy-done.3
  424.8 2.3 convolution_bitcast_fusion
  427.1 159.7 %all-reduce.2.cloned.1.call-done = f32[64,256]{1,0:T(8,128)} async-done(((f32[64,256]{1,0:T(8,128)}), f32[64,256]{1,0:T(8,128)}) %all-reduce.2.cloned.1.call-update) | async-done | bytes 65552 | tf_op jit(solution)/shard_map/psum | solution.py:100
  586.8 1.5 broadcast_multiply_fusion.1
  (10 shorter events, 0.1 us)
Async XLA Ops:
  7.2 1.0 copy-start
  7.2 39.7 %reduce-scatter.2.cloned.1.call-start = ((), (), s32[]{:S(2)}) async-start(), calls=%async_computation.3 | async-start | bytes 2621440 | tf_op jit(solution)/shard_map/reduce_scatter | solution.py:22
  10.7 38.0 %copy-start.5 = (s32[128]{0:T(128)S(1)}, s32[128]{0:T(128)}, u32[]{:S(2)}) copy-start(s32[128]{0:T(128)} %param.9) | copy-start | bytes 1540
  10.7 140.0 %all-gather.3.cloned.1.call-start = ((), (), s32[]{:S(2)}) async-start(), calls=%async_computation.4 | async-start | bytes 17039360 | tf_op jit(solution)/shard_map/all_gather | solution.py:52
  51.0 138.2 %all-to-all-start = ((s32[64,1,2]{2,1,0:T(1,128)}), s32[64,1,2]{2,1,0:T(1,128)S(1)}, u32[]{:S(2)}, u32[]{:S(2)}) async-start(s32[64,1,2]{2,1,0:T(1,128)} %bitcast.17), calls=%async_computation.1 | async-start | bytes 65536 | tf_op jit(solution)/shard_map/all_to_all | solution.py:49
  172.8 2.8 copy-start.1
  175.6 0.9 copy-start.2
  175.6 1.0 copy-start.4
  189.2 102.1 %all-to-all-start.1 = ((f32[64,2,64,128]{3,1,2,0:T(2,128)}), f32[64,2,64,128]{3,1,2,0:T(2,128)}, u32[]{:S(2)}, u32[]{:S(2)}) async-start(f32[64,2,64,128]{3,1,2,0:T(2,128)} %copy.32), calls=%async_computation.2 | async-start | bytes 8388608 | tf_op jit(solution)/shard_map/all_to_all | solution.py:86
  195.4 227.0 %all-gather.5.cloned.1.call-start = ((), (), s32[]{:S(2)}) async-start(), calls=%async_computation.5 | async-start | bytes 1310720 | tf_op jit(solution)/shard_map/all_gather | solution.py:94
  297.3 127.4 %copy-start.3 = (bf16[64,256]{1,0:T(8,128)(2,1)S(1)}, bf16[64,256]{1,0:T(8,128)(2,1)}, u32[]{:S(2)}) copy-start(bf16[64,256]{1,0:T(8,128)(2,1)} %param.7) | copy-start | bytes 98308
  298.1 288.7 %all-reduce.2.cloned.1.call-start = ((), (), s32[]{:S(2)}) async-start(), calls=%async_computation.6 | async-start | bytes 131072 | tf_op jit(solution)/shard_map/psum | solution.py:100
Sparse Core Ops, SparseCore 0:
  10.8 36.0 reduce-scatter.1
  50.7 100.0 all-gather.2
  298.2 21.9 all-gather.4
  424.9 161.8 all-reduce.1
where the time goes:
time: 596 us; the launch traced here: 595 us
  waiting for transfers between devices  374 us (63%)
  blocking collectives  124 us (21%)
  local copies, waits for them, and re-layouts  40.5 us (7%)
  starting transfers between devices  17.1 us (3%)
  matrix products  17 us (3%)
  between operations  14 us (2%)
  other arithmetic  8.64 us (1%)
    psum x1, waiting for transfers between devices, local(): weight_total, bias_total = lax.psum((partial_rows, bias_part), 'rows')  160 us
    psum x1, blocking collectives, local(): weight_total, bias_total = lax.psum((partial_rows, bias_part), 'rows')  124 us
    all_to_all x1, waiting for transfers between devices, local(): lax.all_to_all(outgoing_back, 'rows', split_axis=0, concat_axis=0, tiled=...  89.9 us
    all_gather x1, waiting for transfers between devices, local(): gathered = lax.all_gather(proj, 'rows', axis=1, tiled=True)  88 us
    reduce_scatter x1, waiting for transfers between devices, local(): lax.psum_scatter(lax.dot_general(columns, feats, (((0,), (0,)), ((), ()))...  36.1 us
    reshape x1, local copies, waits for them, and re-layouts, local(): gathered = gathered.reshape(hid_dev, -1, block)  15.3 us
  transfers between devices with their start and end apart: 6, of which 4 were waited for; matrix products, arithmetic and copies ran while one was open for 8% of the time, Pallas kernels for 0%

commit v1 on v0

--- a/solution.py
+++ b/solution.py
@@ -49,7 +49,9 @@
     wanted = lax.all_to_all(
         request.reshape(peers, capacity), "rows", split_axis=0, concat_axis=0, tiled=True
     ).reshape(-1)
-    gathered = lax.all_gather(proj, "rows", axis=1, tiled=True)
+    gathered = jnp.concatenate(
+        lax.all_to_all(jnp.stack([proj] * lax.axis_size("rows")), "rows", 0, 0), axis=1
+    )
     gathered = gathered.reshape(hid_dev, -1, block)
     fetched = jnp.take(gathered, tile_cols, axis=1).reshape(hid_dev, row_blocks, per_block, block)
     local_part = jnp.einsum(

time: 596 us -> 933 us (1.57)
  waiting for transfers between devices: 374 us -> 646 us
  local copies, waits for them, and re-layouts: 40.5 us -> 94 us
  starting transfers between devices: 17.1 us -> 27.9 us
    all_to_all x0 -> x1, waiting for transfers between devices: none -> 362 us  [local(): lax.all_to_all(jnp.stack([proj] * lax.axis_size('rows')), 'rows', 0, 0)]
    all_gather x1 -> x0, waiting for transfers between devices: 88 us -> none  [local(): gathered = lax.all_gather(proj, 'rows', axis=1, tiled=True)]
    another operation x0 -> x3, local copies, waits for them, and re-layouts: none -> 50.2 us  [the longest x2 44.2 us: local(): gathered = gathered.reshape(hid_dev, -1, block)]
    all_to_all x0 -> x1, starting transfers between devices: none -> 11 us  [local(): lax.all_to_all(jnp.stack([proj] * lax.axis_size('rows')), 'rows', 0, 0)]
  transfers between devices with their start and end apart: 6 -> 6, of which waited for: 4 -> 4; matrix products, arithmetic and copies ran while one was open for 8% -> 10% of each run, Pallas kernels for 0% -> 0%
where the time goes in v1:
time: 933 us; the launch traced here: 931 us
  waiting for transfers between devices  646 us (69%)
  blocking collectives  124 us (13%)
  local copies, waits for them, and re-layouts  94 us (10%)
  starting transfers between devices  27.9 us (3%)
  matrix products  17 us (2%)
  between operations  14 us (2%)
    all_to_all x1, waiting for transfers between devices, local(): lax.all_to_all(jnp.stack([proj] * lax.axis_size('rows')), 'rows', 0, 0)  362 us
    psum x1, waiting for transfers between devices, local(): weight_total, bias_total = lax.psum((partial_rows, bias_part), 'rows')  158 us
    psum x1, blocking collectives, local(): weight_total, bias_total = lax.psum((partial_rows, bias_part), 'rows')  124 us
    all_to_all x1, waiting for transfers between devices, local(): lax.all_to_all(outgoing_back, 'rows', split_axis=0, concat_axis=0, tiled=...  89.8 us
    another operation x2, local copies, waits for them, and re-layouts, local(): gathered = gathered.reshape(hid_dev, -1, block)  44.2 us
    reduce_scatter x1, waiting for transfers between devices, local(): lax.psum_scatter(lax.dot_general(columns, feats, (((0,), (0,)), ((), ()))...  36.2 us
  transfers between devices with their start and end apart: 6, of which 4 were waited for; matrix products, arithmetic and copies ran while one was open for 10% of the time, Pallas kernels for 0%

profile of v1, /device:TPU:1, one launch (start us, length us, event | category | flops | bytes accessed | tf_op | source)
XLA Modules:
  0.0 930.7 jit_solution(17372737411794609728)
XLA Ops:
  7.2 0.0 copy-start
  7.2 0.0 reduce-scatter.2.cloned.1.call-start
  7.2 0.9 copy-done
  8.1 2.6 fusion.50
  10.7 0.0 reduce-scatter.2.cloned.1.call-update
  10.7 36.2 %reduce-scatter.2.cloned.1.call-done = f32[64,2048]{1,0:T(8,128)} async-done(((f32[256,2048]{1,0:T(8,128)}), f32[64,2048]{1,0:T(8,128)}) %reduce-scatter.2.cloned.1.call-update) | async-done | bytes 524304 | tf_op jit(solution)/shard_map/reduce_scatter | solution.py:22
  46.9 1.1 convert_element_type.27
  48.0 6.0 stack.2
  54.0 0.0 copy-start.5
  54.0 11.0 %all-to-all-start = ((bf16[64,64,2048]{2,1,0:T(8,128)(2,1)}), bf16[64,64,2048]{2,1,0:T(8,128)(2,1)}, u32[]{:S(2)}, u32[]{:S(2)}) async-start(bf16[64,64,2048]{2,1,0:T(8,128)(2,1)} %stack.2), calls=%async_computation.1 | async-start | bytes 33554432 | tf_op jit(solution)/shard_map/all_to_all | solution.py:53
  64.9 0.0 copy-done.5
  64.9 0.1 reshape.162
  65.0 0.1 fusion.49
  65.1 0.1 reshape.165
  65.2 0.1 reshape.164
  65.3 0.1 broadcast_in_dim.26
  65.4 0.1 fusion.33
  65.5 0.1 reduce_window_sum.11
  65.6 0.2 select_reduce_fusion
  65.8 0.8 scatter_custom_fusion.1
  66.6 0.1 reshape.168
  66.7 0.8 scatter_custom_fusion
  67.5 0.8 all_to_all.13
  68.3 362.2 %all-to-all-done = bf16[64,64,2048]{2,1,0:T(8,128)(2,1)} async-done(((bf16[64,64,2048]{2,1,0:T(8,128)(2,1)}), bf16[64,64,2048]{2,1,0:T(8,128)(2,1)}, u32[]{:S(2)}, u32[]{:S(2)}) %all-to-all-start) | async-done | bytes 16777248 | tf_op jit(solution)/shard_map/all_to_all | solution.py:53
  430.5 6.1 all-to-all-start.1
  436.5 18.6 %copy.26 = bf16[64,64,2048]{2,1,0:T(8,128)(2,1)} copy(bf16[64,64,2048]{2,0,1:T(8,128)(2,1)} %bitcast) | data formatting | bytes 33554432 | tf_op jit(solution)/shard_map/reshape | solution.py:52
  455.2 25.6 %reshape_reshape.3 = bf16[64,1024,128]{2,1,0:T(8,128)(2,1)} reshape(bf16[64,64,2048]{2,1,0:T(8,128)(2,1)} %copy.26) | data formatting | bytes 33554432 | tf_op jit(solution)/shard_map/reshape;reshape | solution.py:55
  480.8 18.6 %copy.27 = bf16[64,1024,128]{2,0,1:T(8,128)(2,1)} copy(bf16[64,1024,128]{2,1,0:T(8,128)(2,1)} %reshape_reshape.3) | data formatting | bytes 33554432 | tf_op jit(solution)/shard_map/reshape;reshape | solution.py:55
  499.4 6.7 gather_fusion
  506.1 0.0 copy-start.1
  506.1 2.6 fusion.16
  508.7 0.2 copy-done.1
  508.9 0.0 copy-start.2
  508.9 0.9 fusion.25
  509.8 0.0 copy-done.2
  509.9 0.0 copy-done.4
  509.9 1.1 fusion.48
  511.0 0.5 fusion.2
  511.5 2.7 gather_fusion.1
  514.2 2.5 broadcast_multiply_fusion
  516.7 5.8 copy.33
  522.5 0.0 all-to-all-done.1
  522.6 10.5 %all-to-all-start.2 = ((f32[64,2,64,128]{3,1,2,0:T(2,128)}), f32[64,2,64,128]{3,1,2,0:T(2,128)}, u32[]{:S(2)}, u32[]{:S(2)}) async-start(f32[64,2,64,128]{3,1,2,0:T(2,128)} %copy.33), calls=%async_computation.3 | async-start | bytes 8388608 | tf_op jit(solution)/shard_map/all_to_all | solution.py:88
  533.1 0.3 all-gather.2.cloned.1.call-start
  533.3 0.1 copy.29
  533.4 0.5 broadcast.165
  533.9 0.7 reduce.3
  534.7 0.1 eq.51
  534.8 2.0 fusion.10
  536.8 2.3 fusion.13
  539.1 89.8 %all-to-all-done.2 = f32[64,2,64,128]{3,1,2,0:T(2,128)} async-done(((f32[64,2,64,128]{3,1,2,0:T(2,128)}), f32[64,2,64,128]{3,1,2,0:T(2,128)}, u32[]{:S(2)}, u32[]{:S(2)}) %all-to-all-start.2) | async-done | bytes 4194336 | tf_op jit(solution)/shard_map/all_to_all | solution.py:88
  629.0 4.5 copy.34
  633.5 1.5 fusion.28
  635.0 0.8 copy.61
  635.8 0.0 all-gather.2.cloned.1.call-update
  635.8 0.0 all-reduce.2.cloned.1.call-start
  635.8 123.7 %psum.15 = f32[64]{0:T(128)S(1)} all-reduce(f32[64]{0:T(128)S(1)} %get-tuple-element.4), channel_id=1, replica_groups=mesh['rows'=64,'feat'=4] {'rows'}, use_global_device_ids=true, to_apply=%region_7.8 | all-reduce | flops 64 | bytes 512 | tf_op jit(solution)/shard_map/psum | solution.py:102
  759.6 0.5 broadcast_multiply_fusion.2
  760.1 2.3 convolution_bitcast_fusion.1
  762.4 0.0 all-reduce.2.cloned.1.call-update
  762.4 0.0 copy-done.3
  762.4 2.3 convolution_bitcast_fusion
  764.8 158.0 %all-reduce.2.cloned.1.call-done = f32[64,256]{1,0:T(8,128)} async-done(((f32[64,256]{1,0:T(8,128)}), f32[64,256]{1,0:T(8,128)}) %all-reduce.2.cloned.1.call-update) | async-done | bytes 65552 | tf_op jit(solution)/shard_map/psum | solution.py:102
  922.7 1.5 broadcast_multiply_fusion.1
  (12 shorter events, 0.1 us)
Async XLA Ops:
  7.2 1.0 copy-start
  7.2 39.7 %reduce-scatter.2.cloned.1.call-start = ((), (), s32[]{:S(2)}) async-start(), calls=%async_computation.4 | async-start | bytes 2621440 | tf_op jit(solution)/shard_map/reduce_scatter | solution.py:22
  54.0 11.0 %copy-start.5 = (s32[128]{0:T(128)S(1)}, s32[128]{0:T(128)}, u32[]{:S(2)}) copy-start(s32[128]{0:T(128)} %param.9) | copy-start | bytes 1540
  54.0 376.5 %all-to-all-start = ((bf16[64,64,2048]{2,1,0:T(8,128)(2,1)}), bf16[64,64,2048]{2,1,0:T(8,128)(2,1)}, u32[]{:S(2)}, u32[]{:S(2)}) async-start(bf16[64,64,2048]{2,1,0:T(8,128)(2,1)} %stack.2), calls=%async_computation.1 | async-start | bytes 33554432 | tf_op jit(solution)/shard_map/all_to_all | solution.py:53
  430.5 92.1 %all-to-all-start.1 = ((s32[64,1,2]{2,1,0:T(1,128)}), s32[64,1,2]{2,1,0:T(1,128)S(1)}, u32[]{:S(2)}, u32[]{:S(2)}) async-start(s32[64,1,2]{2,1,0:T(1,128)} %bitcast.18), calls=%async_computation.2 | async-start | bytes 65536 | tf_op jit(solution)/shard_map/all_to_all | solution.py:49
  506.1 2.8 copy-start.1
  508.9 0.9 copy-start.2
  508.9 1.0 copy-start.4
  522.6 106.4 %all-to-all-start.2 = ((f32[64,2,64,128]{3,1,2,0:T(2,128)}), f32[64,2,64,128]{3,1,2,0:T(2,128)}, u32[]{:S(2)}, u32[]{:S(2)}) async-start(f32[64,2,64,128]{3,1,2,0:T(2,128)} %copy.33), calls=%async_computation.3 | async-start | bytes 8388608 | tf_op jit(solution)/shard_map/all_to_all | solution.py:88
  533.1 227.0 %all-gather.2.cloned.1.call-start = ((), (), s32[]{:S(2)}) async-start(), calls=%async_computation.5 | async-start | bytes 1310720 | tf_op jit(solution)/shard_map/all_gather | solution.py:96
  635.0 127.4 %copy-start.3 = (bf16[64,256]{1,0:T(8,128)(2,1)S(1)}, bf16[64,256]{1,0:T(8,128)(2,1)}, u32[]{:S(2)}) copy-start(bf16[64,256]{1,0:T(8,128)(2,1)} %param.7) | copy-start | bytes 98308
  635.8 286.9 %all-reduce.2.cloned.1.call-start = ((), (), s32[]{:S(2)}) async-start(), calls=%async_computation.6 | async-start | bytes 131072 | tf_op jit(solution)/shard_map/psum | solution.py:102
Sparse Core Ops, SparseCore 0:
  10.8 36.0 reduce-scatter.1
  635.9 20.4 all-gather.1
  762.6 160.1 all-reduce.1
